TPU v7x, 32 devices: a whole 2x2x4 slice. The times are simulated.
32 devices in a mesh: row: 4 (over z), col: 2 (over y), depth: 4 (over x, core).
Axes of the slice: x: 2, y: 2, z: 4, core: 2. Of those that a mesh axis runs over, the one named last changes fastest.
Arguments:
- right_sides: float32 [64, 4096], P('depth', ('row', 'col')), may hold values from -12 to 12
- blocks: float32 [4, 2, 16, 256, 256], P('row', 'col'), may hold values from -0.06 to 6.1, as said below
- block_rows: int32 [4, 2, 16], P('row', 'col'), may hold values from 0 to 3, as said below
- block_cols: int32 [4, 2, 16], P('row', 'col'), may hold values from 0 to 7, as said below
- block_count: int32 [4, 2], P('row', 'col'), may hold values from 2 to 16
Outputs:
- solution: float32 [64, 4096], P('depth', ('row', 'col'))
- residual: float32 [64, 4096], P('depth', ('row', 'col'))
Inputs may be any that keep to these rules, and one draw needn't show every extreme that they name: Slot s < 2 of row index r and col index c holds the diagonal block with block_rows = c * 2 + s and block_cols = r * 2 + s. The valid later slots name distinct blocks whose I is below J. At slots from block_count on, block_rows and block_cols hold 0; blocks there hold arbitrary values and are not part of A. `block_cols`: see block_rows. Diagonal-slot blocks are symmetric; A is positive definite. Slots from block_count on are not part of A.
All inputs are finite; a program needn't handle non-finite values.
Results may differ from a plain program's by a relative error of at most 0.0003.
Values sent between devices are 32-bit elements; how exact they have to be, the bound alone decides.
No kernel may reach another device: no remote copies, remote signals or barrier semaphores. Data moves between devices by JAX's collectives and lax.ppermute only.
A program may use at most 64 MiB of HBM per device.

v0:
```python
import jax
import jax.numpy as jnp
from jax import lax
from jax.sharding import PartitionSpec as P

BLK = 256
ITERS = 2
SEG = 2


def per_device(right_sides, blocks, block_rows, block_cols, block_count):
    highest = lax.Precision.HIGHEST
    own_width = right_sides.shape[0]
    depth_index = lax.axis_index("depth")
    tile_blocks = blocks[0, 0]
    rows_here = block_rows[0, 0]
    cols_here = block_cols[0, 0]
    live_count = block_count[0, 0]
    row_span = SEG * lax.axis_size("col")
    col_span = SEG * lax.axis_size("row")
    slot_index = jnp.arange(tile_blocks.shape[0], dtype=jnp.int32)
    residual_all = lax.all_gather(right_sides, "depth", axis=0, tiled=True)
    direction_all = residual_all
    solution = jnp.zeros_like(right_sides)
    current = lax.psum(jnp.dot(residual_all, residual_all.T, precision=highest), ("row", "col"))
    for iteration in range(ITERS):
        own_direction = lax.dynamic_slice_in_dim(
            direction_all, depth_index * own_width, own_width, 0
        )
        row_part = lax.all_gather(own_direction, "col", axis=1, tiled=True).reshape(
            own_width, row_span, BLK
        )
        col_part = lax.all_gather(own_direction, "row", axis=1, tiled=True).reshape(
            own_width, col_span, BLK
        )
        live_mask = (slot_index < live_count).astype(jnp.float32)
        mirror_mask = live_mask * (slot_index >= SEG).astype(jnp.float32)
        toward_rows = jnp.einsum(
            "csk,smk->csm", col_part[:, cols_here], tile_blocks, precision=highest
        )
        toward_cols = jnp.einsum(
            "csm,smk->csk", row_part[:, rows_here], tile_blocks, precision=highest
        )
        toward_rows = toward_rows * live_mask[None, :, None]
        toward_cols = toward_cols * mirror_mask[None, :, None]
        row_select = (rows_here[:, None] == jnp.arange(row_span, dtype=jnp.int32)[None, :]).astype(
            jnp.float32
        )
        col_select = (cols_here[:, None] == jnp.arange(col_span, dtype=jnp.int32)[None, :]).astype(
            jnp.float32
        )
        row_terms = jnp.einsum("si,csm->cim", row_select, toward_rows, precision=highest)
        col_terms = jnp.einsum("sj,csk->cjk", col_select, toward_cols, precision=highest)
        row_sum = lax.psum_scatter(
            row_terms.reshape(own_width, row_span * BLK), "col", scatter_dimension=1, tiled=True
        )
        col_sum = lax.psum_scatter(
            col_terms.reshape(own_width, col_span * BLK), "row", scatter_dimension=1, tiled=True
        )
        mapped = row_sum + col_sum
        mapped_all = lax.all_gather(mapped, "depth", axis=0, tiled=True)
        curvature, cross_gram, image_gram = lax.psum(
            (
                jnp.dot(direction_all, mapped_all.T, precision=highest),
                jnp.dot(residual_all, mapped_all.T, precision=highest),
                jnp.dot(mapped_all, mapped_all.T, precision=highest),
            ),
            ("row", "col"),
        )
        step_size = jax.scipy.linalg.cho_solve((jnp.linalg.cholesky(curvature), True), current)
        own_step = lax.dynamic_slice_in_dim(step_size, depth_index * own_width, own_width, 1)
        solution = solution + lax.dot_general(
            own_step, direction_all, (((0,), (0,)), ((), ())), precision=highest
        )
        residual_all = residual_all - lax.dot_general(
            step_size, mapped_all, (((0,), (0,)), ((), ())), precision=highest
        )
        if iteration + 1 < ITERS:
            coupling = jnp.dot(cross_gram, step_size, precision=highest)
            quadratic = lax.dot_general(
                step_size,
                jnp.dot(image_gram, step_size, precision=highest),
                (((0,), (0,)), ((), ())),
                precision=highest,
            )
            renewed = current - coupling - coupling.T + quadratic
            conjugate = jax.scipy.linalg.cho_solve((jnp.linalg.cholesky(current), True), renewed)
            direction_all = residual_all + lax.dot_general(
                conjugate, direction_all, (((0,), (0,)), ((), ())), precision=highest
            )
            current = renewed
    own_residual = lax.dynamic_slice_in_dim(residual_all, depth_index * own_width, own_width, 0)
    return (solution, own_residual)


def solution(mesh):
    return jax.shard_map(
        per_device,
        mesh=mesh,
        in_specs=(
            P("depth", ("row", "col")),
            P("row", "col", None, None, None),
            P("row", "col", None),
            P("row", "col", None),
            P("row", "col"),
        ),
        out_specs=(P("depth", ("row", "col")), P("depth", ("row", "col"))),
        check_vma=False,
    )
```

profile of v0, /device:TPU:0, one launch (start us, length us, event | category | flops | bytes accessed | tf_op | source)
XLA Modules:
  0.0 254.3 jit_solution(11665464484053111125)
XLA Ops:
  7.2 6.7 %all_gather.21 = f32[64,512]{1,0:T(8,128)S(1)} all-gather(f32[16,512]{1,0:T(8,128)} %param.8), channel_id=1, replica_groups=mesh['row'=4,'col'=2,'depth'=4] {'depth'}, dimensions={0}, use_global_device_ids=true | all-gather | bytes 163840 | tf_op jit(solution)/shard_map/all_gather | solution.py:22
  13.9 13.9 %all_gather.22 = f32[16,2048]{1,0:T(8,128)S(1)} all-gather(f32[16,512]{1,0:T(8,128)S(1)} %constant_dynamic-slice_fusion.1), channel_id=1, replica_groups=mesh['row'=4,'col'=2,'depth'=4] {'row'}, dimensions={1}, use_global_device_ids=true | all-gather | bytes 163840 | tf_op jit(solution)/shard_map/all_gather | solution.py:33
  29.8 5.7 %fusion.6 = f32[16,16,256]{2,1,0:T(8,128)S(1)} fusion(f32[1,1,16,256,256]{4,3,2,1,0:T(8,128)} %param.9, f32[16,16,256]{2,1,0:T(8,128)S(1)} %gather_fusion), kind=kOutput, calls=%fused_computation.10 | convolution fusion | flops 201326592 | bytes 4718592 | tf_op jit(solution)/shard_map/csk,smk->csm/dot_general | solution.py:38
  36.6 4.6 %all_gather.23 = f32[16,1024]{1,0:T(8,128)S(1)} all-gather(f32[16,512]{1,0:T(8,128)S(1)} %constant_dynamic-slice_fusion.1), channel_id=1, replica_groups=mesh['row'=4,'col'=2,'depth'=4] {'col'}, dimensions={1}, use_global_device_ids=true | all-gather | bytes 98304 | tf_op jit(solution)/shard_map/all_gather | solution.py:30
  41.8 4.3 %fusion.4 = f32[16,16,256]{2,1,0:T(8,128)S(1)} fusion(f32[1,1,16,256,256]{4,3,2,1,0:T(8,128)} %param.9, f32[16,16,256]{2,1,0:T(8,128)S(1)} %gather_fusion.1), kind=kOutput, calls=%fused_computation.8 | convolution fusion | flops 201326592 | bytes 4718592 | tf_op jit(solution)/shard_map/csm,smk->csk/dot_general | solution.py:41
  47.8 21.8 %reduce-scatter.7.cloned.1.call-done = f32[16,512]{1,0:T(8,128)} async-done(((f32[16,2048]{1,0:T(8,128)}), f32[16,512]{1,0:T(8,128)}) %reduce-scatter.7.cloned.1.call-update) | async-done | bytes 32784 | tf_op jit(solution)/shard_map/reduce_scatter | solution.py:57
  69.6 0.8 add.75
  70.4 5.4 %all_gather.24 = f32[64,512]{1,0:T(8,128)S(1)} all-gather(f32[16,512]{1,0:T(8,128)S(1)} %add.75), channel_id=1, replica_groups=mesh['row'=4,'col'=2,'depth'=4] {'depth'}, dimensions={0}, use_global_device_ids=true | all-gather | bytes 163840 | tf_op jit(solution)/shard_map/all_gather | solution.py:61
  76.3 35.3 %all-reduce = (f32[64,64]{0,1:T(8,128)S(1)}, f32[64,64]{0,1:T(8,128)S(1)}, f32[64,64]{1,0:T(8,128)S(1)}) all-reduce(f32[64,64]{0,1:T(8,128)S(1)} %fusion.59, f32[64,64]{0,1:T(8,128)S(1)} %convolution_bitcast_fusion, f32[64,64]{1,0:T(8,128)S(1)} %fusion.61), channel_id=1, replica_groups=mesh['row'=4,'col'=2,'depth'=4] {'row','col'}, use_global_device_ids=true, to_apply=%region_5.7 | all-reduce | flops 12288 | bytes 98304 | tf_op jit(solution)/shard_map/psum | solution.py:25
  111.8 5.8 %cholesky.59 = f32[64,64]{1,0:T(8,128)S(1)} custom-call(f32[64,64]{1,0:T(8,128)S(1)} %get-tuple-element.8), custom_call_target="Cholesky" | custom-call | tf_op jit(solution)/shard_map/jit(cholesky)/cholesky | solution.py:70
  119.0 4.9 %custom-call.9 = f32[1,64,64]{1,2,0:T(8,128)S(1)} custom-call(f32[1,64,64]{2,1,0:T(8,128)S(1)} %fusion.24), custom_call_target="InvertDiagBlocksLowerTriangular" | custom-call | tf_op jit(solution)/shard_map/jit(_cho_solve)/triangular_solve | solution.py:70
  125.2 5.9 %cholesky.70 = f32[64,64]{1,0:T(8,128)S(1)} custom-call(f32[64,64]{1,0:T(8,128)S(1)} %get-tuple-element.7), custom_call_target="Cholesky" | custom-call | tf_op jit(solution)/shard_map/jit(cholesky)/cholesky | solution.py:87
  132.4 4.9 %custom-call.10 = f32[1,64,64]{1,2,0:T(8,128)S(1)} custom-call(f32[1,64,64]{2,1,0:T(8,128)S(1)} %fusion.25), custom_call_target="InvertDiagBlocksLowerTriangular" | custom-call | tf_op jit(solution)/shard_map/jit(_cho_solve)/triangular_solve | solution.py:87
  138.3 13.3 %all_gather.25 = f32[16,2048]{1,0:T(8,128)S(1)} all-gather(f32[16,512]{1,0:T(8,128)S(1)} %constant_dynamic-slice_fusion), channel_id=1, replica_groups=mesh['row'=4,'col'=2,'depth'=4] {'row'}, dimensions={1}, use_global_device_ids=true | all-gather | bytes 163840 | tf_op jit(solution)/shard_map/all_gather | solution.py:33
  151.6 4.6 %all_gather.26 = f32[16,1024]{1,0:T(8,128)S(1)} all-gather(f32[16,512]{1,0:T(8,128)S(1)} %constant_dynamic-slice_fusion), channel_id=1, replica_groups=mesh['row'=4,'col'=2,'depth'=4] {'col'}, dimensions={1}, use_global_device_ids=true | all-gather | bytes 98304 | tf_op jit(solution)/shard_map/all_gather | solution.py:30
  156.8 5.7 %fusion.2 = f32[16,16,256]{2,1,0:T(8,128)S(1)} fusion(f32[1,1,16,256,256]{4,3,2,1,0:T(8,128)} %param.9, f32[16,16,256]{2,1,0:T(8,128)S(1)} %gather_fusion.2), kind=kOutput, calls=%fused_computation.6 | convolution fusion | flops 201326592 | bytes 4718592 | tf_op jit(solution)/shard_map/csk,smk->csm/dot_general | solution.py:38
  164.2 4.3 %fusion = f32[16,16,256]{2,1,0:T(8,128)S(1)} fusion(f32[1,1,16,256,256]{4,3,2,1,0:T(8,128)} %param.9, f32[16,16,256]{2,1,0:T(8,128)S(1)} %gather_fusion.3), kind=kOutput, calls=%fused_computation.4 | convolution fusion | flops 201326592 | bytes 4718592 | tf_op jit(solution)/shard_map/csm,smk->csk/dot_general | solution.py:41
  169.7 1.3 reduce-scatter.9.cloned.1.call-done
  171.0 21.6 %reduce-scatter.11.cloned.1.call-done = f32[16,512]{1,0:T(8,128)} async-done(((f32[16,2048]{1,0:T(8,128)}), f32[16,512]{1,0:T(8,128)}) %reduce-scatter.11.cloned.1.call-update) | async-done | bytes 32784 | tf_op jit(solution)/shard_map/reduce_scatter | solution.py:57
  193.4 5.4 %all_gather.27 = f32[64,512]{1,0:T(8,128)S(1)} all-gather(f32[16,512]{1,0:T(8,128)S(1)} %add.78), channel_id=1, replica_groups=mesh['row'=4,'col'=2,'depth'=4] {'depth'}, dimensions={0}, use_global_device_ids=true | all-gather | bytes 163840 | tf_op jit(solution)/shard_map/all_gather | solution.py:61
  199.1 34.3 %psum.34 = f32[64,64]{0,1:T(8,128)S(1)} all-reduce(f32[64,64]{0,1:T(8,128)S(1)} %fusion.63), channel_id=1, replica_groups=mesh['row'=4,'col'=2,'depth'=4] {'row','col'}, use_global_device_ids=true, to_apply=%region_9.12 | all-reduce | flops 4096 | bytes 32768 | tf_op jit(solution)/shard_map/psum | solution.py:62
  233.5 5.8 %cholesky.81 = f32[64,64]{1,0:T(8,128)S(1)} custom-call(f32[64,64]{1,0:T(8,128)S(1)} %fusion.31), custom_call_target="Cholesky" | custom-call | tf_op jit(solution)/shard_map/jit(cholesky)/cholesky | solution.py:70
  240.7 4.9 %custom-call.11 = f32[1,64,64]{1,2,0:T(8,128)S(1)} custom-call(f32[1,64,64]{2,1,0:T(8,128)S(1)} %fusion.26), custom_call_target="InvertDiagBlocksLowerTriangular" | custom-call | tf_op jit(solution)/shard_map/jit(_cho_solve)/triangular_solve | solution.py:70
  246.3 0.8 convolution_add_fusion.1
  (71 shorter events, 17.4 us)
Async XLA Ops:
  7.2 28.4 %copy-start = (s32[1,1,16]{2,1,0:T(1,128)S(1)}, s32[1,1,16]{2,1,0:T(1,128)}, u32[]{:S(2)}) copy-start(s32[1,1,16]{2,1,0:T(1,128)} %param.10) | copy-start | bytes 196
  7.2 40.7 %reduce-scatter.5.cloned.1.call-start = ((), (), s32[]{:S(2)}) async-start(), calls=%async_computation.4 | async-start | bytes 98304 | tf_op jit(solution)/shard_map/reduce_scatter | solution.py:54
  29.8 16.3 %copy-start.1 = (s32[1,1,16]{2,1,0:T(1,128)S(1)}, s32[1,1,16]{2,1,0:T(1,128)}, u32[]{:S(2)}) copy-start(s32[1,1,16]{2,1,0:T(1,128)} %param.11) | copy-start | bytes 196
  36.6 33.0 %reduce-scatter.7.cloned.1.call-start = ((), (), s32[]{:S(2)}) async-start(), calls=%async_computation.5 | async-start | bytes 163840 | tf_op jit(solution)/shard_map/reduce_scatter | solution.py:57
  47.2 123.8 %reduce-scatter.9.cloned.1.call-start = ((), (), s32[]{:S(2)}) async-start(), calls=%async_computation.6 | async-start | bytes 98304 | tf_op jit(solution)/shard_map/reduce_scatter | solution.py:54
  163.5 29.1 %reduce-scatter.11.cloned.1.call-start = ((), (), s32[]{:S(2)}) async-start(), calls=%async_computation.7 | async-start | bytes 163840 | tf_op jit(solution)/shard_map/reduce_scatter | solution.py:57
Sparse Core Ops, SparseCore 0:
  36.7 11.1 reduce-scatter.4
  50.1 19.4 reduce-scatter.6
  163.6 7.3 reduce-scatter.8
  173.1 19.4 reduce-scatter.10
where the time goes:
time: 255 us; the launch traced here: 254 us
  blocking collectives  124 us (49%)
  waiting for transfers between devices  45 us (18%)
  other arithmetic  39.1 us (15%)
  matrix products  26.4 us (10%)
  between operations  14.8 us (6%)
  local copies, waits for them, and re-layouts  5.25 us (2%)
    reduce_scatter x2, waiting for transfers between devices, per_device(): lax.psum_scatter(col_terms.reshape(own_width, col_span * BLK), 'row', sca...  43.4 us
    psum x1, blocking collectives, per_device(): lax.psum(jnp.dot(residual_all, residual_all.T, precision=highest), ('row'...  35.3 us
    psum x1, blocking collectives, per_device(): lax.psum((jnp.dot(direction_all, mapped_all.T, precision=highest), jnp.do...  34.3 us
    all_gather x2, blocking collectives, per_device(): lax.all_gather(own_direction, 'row', axis=1, tiled=True)  27.3 us
    another operation x6, other arithmetic, per_device(): jnp.linalg.cholesky(curvature)  13 us
    dot_general x2, matrix products, per_device(): jnp.einsum('csk,smk->csm', col_part[:, cols_here], tile_blocks, precision...  11.4 us
    another operation x4, other arithmetic, per_device(): jax.scipy.linalg.cho_solve((jnp.linalg.cholesky(curvature), True), current)  11.1 us
    all_gather x2, blocking collectives, per_device(): mapped_all = lax.all_gather(mapped, 'depth', axis=0, tiled=True)  10.8 us
  transfers between devices with their start and end apart: 4, of which 4 were waited for; matrix products, arithmetic and copies ran while one was open for 5% of the time, Pallas kernels for 0%

commit v1 on v0

--- a/solution.py
+++ b/solution.py
@@ -6,6 +6,11 @@
 BLK = 256
 ITERS = 2
 SEG = 2
+
+
+def all_parts(value, axis, along):
+    shards = lax.all_gather(value, axis)
+    return jnp.concatenate(shards, axis=along)
 
 
 def per_device(right_sides, blocks, block_rows, block_cols, block_count):
@@ -30,9 +35,7 @@
         row_part = lax.all_gather(own_direction, "col", axis=1, tiled=True).reshape(
             own_width, row_span, BLK
         )
-        col_part = lax.all_gather(own_direction, "row", axis=1, tiled=True).reshape(
-            own_width, col_span, BLK
-        )
+        col_part = all_parts(own_direction, "row", 1).reshape(own_width, col_span, BLK)
         live_mask = (slot_index < live_count).astype(jnp.float32)
         mirror_mask = live_mask * (slot_index >= SEG).astype(jnp.float32)
         toward_rows = jnp.einsum(

time: 255 us -> 255 us (level)
  no operation moved by 1% of the time
where the time goes in v1:
time: 255 us
  blocking collectives  124 us (49%)
  waiting for transfers between devices  45 us (18%)
  other arithmetic  39.1 us (15%)
  matrix products  26.4 us (10%)
  between operations  14.8 us (6%)
  local copies, waits for them, and re-layouts  5.6 us (2%)
    reduce_scatter x2, waiting for transfers between devices, per_device(): lax.psum_scatter(col_terms.reshape(own_width, col_span * BLK), 'row', sca...  43.3 us
    psum x1, blocking collectives, per_device(): lax.psum(jnp.dot(residual_all, residual_all.T, precision=highest), ('row'...  35.3 us
    psum x1, blocking collectives, per_device(): lax.psum((jnp.dot(direction_all, mapped_all.T, precision=highest), jnp.do...  34.5 us
    all_gather x2, blocking collectives, all_parts(): shards = lax.all_gather(value, axis)  27.3 us
    another operation x6, other arithmetic, per_device(): jnp.linalg.cholesky(curvature)  13 us
    dot_general x2, matrix products, per_device(): jnp.einsum('csk,smk->csm', col_part[:, cols_here], tile_blocks, precision...  11.4 us
    another operation x4, other arithmetic, per_device(): jax.scipy.linalg.cho_solve((jnp.linalg.cholesky(curvature), True), current)  11.1 us
    all_gather x2, blocking collectives, per_device(): mapped_all = lax.all_gather(mapped, 'depth', axis=0, tiled=True)  10.8 us
  transfers between devices with their start and end apart: 4, of which 4 were waited for; matrix products, arithmetic and copies ran while one was open for 5% of the time, Pallas kernels for 0%

profile of v1, /device:TPU:0, one launch (start us, length us, event | category | flops | bytes accessed | tf_op | source)
XLA Modules:
  0.0 254.8 jit_solution(4442863936200090541)
XLA Ops:
  7.2 6.7 %all_gather.27 = f32[64,512]{1,0:T(8,128)S(1)} all-gather(f32[16,512]{1,0:T(8,128)} %param.8), channel_id=1, replica_groups=mesh['row'=4,'col'=2,'depth'=4] {'depth'}, dimensions={0}, use_global_device_ids=true | all-gather | bytes 163840 | tf_op jit(solution)/shard_map/all_gather | solution.py:27
  13.9 13.9 %all-gather = f32[64,512]{1,0:T(8,128)S(1)} all-gather(f32[16,512]{1,0:T(8,128)S(1)} %constant_dynamic-slice_fusion.1), channel_id=2, replica_groups=mesh['row'=4,'col'=2,'depth'=4] {'row'}, dimensions={0}, use_global_device_ids=true | all-gather | bytes 163840 | tf_op jit(solution)/shard_map/all_gather | solution.py:12
  30.0 5.7 %fusion.6 = f32[16,16,256]{2,1,0:T(8,128)S(1)} fusion(f32[1,1,16,256,256]{4,3,2,1,0:T(8,128)} %param.9, f32[16,16,256]{2,1,0:T(8,128)S(1)} %gather_fusion), kind=kOutput, calls=%fused_computation.10 | convolution fusion | flops 201326592 | bytes 4718592 | tf_op jit(solution)/shard_map/csk,smk->csm/dot_general | solution.py:41
  36.8 4.6 %all_gather.30 = f32[16,1024]{1,0:T(8,128)S(1)} all-gather(f32[16,512]{1,0:T(8,128)S(1)} %constant_dynamic-slice_fusion.1), channel_id=1, replica_groups=mesh['row'=4,'col'=2,'depth'=4] {'col'}, dimensions={1}, use_global_device_ids=true | all-gather | bytes 98304 | tf_op jit(solution)/shard_map/all_gather | solution.py:35
  42.0 4.3 %fusion.4 = f32[16,16,256]{2,1,0:T(8,128)S(1)} fusion(f32[1,1,16,256,256]{4,3,2,1,0:T(8,128)} %param.9, f32[16,16,256]{2,1,0:T(8,128)S(1)} %gather_fusion.1), kind=kOutput, calls=%fused_computation.8 | convolution fusion | flops 201326592 | bytes 4718592 | tf_op jit(solution)/shard_map/csm,smk->csk/dot_general | solution.py:44
  48.0 21.8 %reduce-scatter.7.cloned.1.call-done = f32[16,512]{1,0:T(8,128)} async-done(((f32[16,2048]{1,0:T(8,128)}), f32[16,512]{1,0:T(8,128)}) %reduce-scatter.7.cloned.1.call-update) | async-done | bytes 32784 | tf_op jit(solution)/shard_map/reduce_scatter | solution.py:60
  69.8 0.8 add.75
  70.6 5.4 %all_gather.31 = f32[64,512]{1,0:T(8,128)S(1)} all-gather(f32[16,512]{1,0:T(8,128)S(1)} %add.75), channel_id=1, replica_groups=mesh['row'=4,'col'=2,'depth'=4] {'depth'}, dimensions={0}, use_global_device_ids=true | all-gather | bytes 163840 | tf_op jit(solution)/shard_map/all_gather | solution.py:64
  76.5 35.3 %all-reduce = (f32[64,64]{0,1:T(8,128)S(1)}, f32[64,64]{0,1:T(8,128)S(1)}, f32[64,64]{1,0:T(8,128)S(1)}) all-reduce(f32[64,64]{0,1:T(8,128)S(1)} %fusion.59, f32[64,64]{0,1:T(8,128)S(1)} %convolution_bitcast_fusion, f32[64,64]{1,0:T(8,128)S(1)} %fusion.61), channel_id=1, replica_groups=mesh['row'=4,'col'=2,'depth'=4] {'row','col'}, use_global_device_ids=true, to_apply=%region_5.7 | all-reduce | flops 12288 | bytes 98304 | tf_op jit(solution)/shard_map/psum | solution.py:30
  112.0 5.8 %cholesky.59 = f32[64,64]{1,0:T(8,128)S(1)} custom-call(f32[64,64]{1,0:T(8,128)S(1)} %get-tuple-element.8), custom_call_target="Cholesky" | custom-call | tf_op jit(solution)/shard_map/jit(cholesky)/cholesky | solution.py:73
  119.2 4.9 %custom-call.9 = f32[1,64,64]{1,2,0:T(8,128)S(1)} custom-call(f32[1,64,64]{2,1,0:T(8,128)S(1)} %fusion.24), custom_call_target="InvertDiagBlocksLowerTriangular" | custom-call | tf_op jit(solution)/shard_map/jit(_cho_solve)/triangular_solve | solution.py:73
  125.4 5.9 %cholesky.70 = f32[64,64]{1,0:T(8,128)S(1)} custom-call(f32[64,64]{1,0:T(8,128)S(1)} %get-tuple-element.7), custom_call_target="Cholesky" | custom-call | tf_op jit(solution)/shard_map/jit(cholesky)/cholesky | solution.py:90
  132.6 4.9 %custom-call.10 = f32[1,64,64]{1,2,0:T(8,128)S(1)} custom-call(f32[1,64,64]{2,1,0:T(8,128)S(1)} %fusion.25), custom_call_target="InvertDiagBlocksLowerTriangular" | custom-call | tf_op jit(solution)/shard_map/jit(_cho_solve)/triangular_solve | solution.py:90
  138.5 13.3 %all-gather.1 = f32[64,512]{1,0:T(8,128)S(1)} all-gather(f32[16,512]{1,0:T(8,128)S(1)} %constant_dynamic-slice_fusion), channel_id=3, replica_groups=mesh['row'=4,'col'=2,'depth'=4] {'row'}, dimensions={0}, use_global_device_ids=true | all-gather | bytes 163840 | tf_op jit(solution)/shard_map/all_gather | solution.py:12
  151.8 4.6 %all_gather.34 = f32[16,1024]{1,0:T(8,128)S(1)} all-gather(f32[16,512]{1,0:T(8,128)S(1)} %constant_dynamic-slice_fusion), channel_id=1, replica_groups=mesh['row'=4,'col'=2,'depth'=4] {'col'}, dimensions={1}, use_global_device_ids=true | all-gather | bytes 98304 | tf_op jit(solution)/shard_map/all_gather | solution.py:35
  157.2 5.7 %fusion.2 = f32[16,16,256]{2,1,0:T(8,128)S(1)} fusion(f32[1,1,16,256,256]{4,3,2,1,0:T(8,128)} %param.9, f32[16,16,256]{2,1,0:T(8,128)S(1)} %gather_fusion.2), kind=kOutput, calls=%fused_computation.6 | convolution fusion | flops 201326592 | bytes 4718592 | tf_op jit(solution)/shard_map/csk,smk->csm/dot_general | solution.py:41
  164.5 4.3 %fusion = f32[16,16,256]{2,1,0:T(8,128)S(1)} fusion(f32[1,1,16,256,256]{4,3,2,1,0:T(8,128)} %param.9, f32[16,16,256]{2,1,0:T(8,128)S(1)} %gather_fusion.3), kind=kOutput, calls=%fused_computation.4 | convolution fusion | flops 201326592 | bytes 4718592 | tf_op jit(solution)/shard_map/csm,smk->csk/dot_general | solution.py:44
  170.1 1.3 reduce-scatter.9.cloned.1.call-done
  171.4 21.6 %reduce-scatter.11.cloned.1.call-done = f32[16,512]{1,0:T(8,128)} async-done(((f32[16,2048]{1,0:T(8,128)}), f32[16,512]{1,0:T(8,128)}) %reduce-scatter.11.cloned.1.call-update) | async-done | bytes 32784 | tf_op jit(solution)/shard_map/reduce_scatter | solution.py:60
  193.7 5.4 %all_gather.35 = f32[64,512]{1,0:T(8,128)S(1)} all-gather(f32[16,512]{1,0:T(8,128)S(1)} %add.78), channel_id=1, replica_groups=mesh['row'=4,'col'=2,'depth'=4] {'depth'}, dimensions={0}, use_global_device_ids=true | all-gather | bytes 163840 | tf_op jit(solution)/shard_map/all_gather | solution.py:64
  199.4 34.5 %psum.34 = f32[64,64]{0,1:T(8,128)S(1)} all-reduce(f32[64,64]{0,1:T(8,128)S(1)} %fusion.63), channel_id=1, replica_groups=mesh['row'=4,'col'=2,'depth'=4] {'row','col'}, use_global_device_ids=true, to_apply=%region_9.12 | all-reduce | flops 4096 | bytes 32768 | tf_op jit(solution)/shard_map/psum | solution.py:65
  234.0 5.8 %cholesky.81 = f32[64,64]{1,0:T(8,128)S(1)} custom-call(f32[64,64]{1,0:T(8,128)S(1)} %fusion.31), custom_call_target="Cholesky" | custom-call | tf_op jit(solution)/shard_map/jit(cholesky)/cholesky | solution.py:73
  241.2 4.9 %custom-call.11 = f32[1,64,64]{1,2,0:T(8,128)S(1)} custom-call(f32[1,64,64]{2,1,0:T(8,128)S(1)} %fusion.26), custom_call_target="InvertDiagBlocksLowerTriangular" | custom-call | tf_op jit(solution)/shard_map/jit(_cho_solve)/triangular_solve | solution.py:73
  246.9 0.8 convolution_add_fusion.1
  (75 shorter events, 17.8 us)
Async XLA Ops:
  7.2 28.6 %copy-start = (s32[1,1,16]{2,1,0:T(1,128)S(1)}, s32[1,1,16]{2,1,0:T(1,128)}, u32[]{:S(2)}) copy-start(s32[1,1,16]{2,1,0:T(1,128)} %param.10) | copy-start | bytes 196
  7.2 40.9 %reduce-scatter.5.cloned.1.call-start = ((), (), s32[]{:S(2)}) async-start(), calls=%async_computation.4 | async-start | bytes 98304 | tf_op jit(solution)/shard_map/reduce_scatter | solution.py:57
  30.0 16.3 %copy-start.1 = (s32[1,1,16]{2,1,0:T(1,128)S(1)}, s32[1,1,16]{2,1,0:T(1,128)}, u32[]{:S(2)}) copy-start(s32[1,1,16]{2,1,0:T(1,128)} %param.11) | copy-start | bytes 196
  36.7 33.0 %reduce-scatter.7.cloned.1.call-start = ((), (), s32[]{:S(2)}) async-start(), calls=%async_computation.5 | async-start | bytes 163840 | tf_op jit(solution)/shard_map/reduce_scatter | solution.py:60
  47.4 124.0 %reduce-scatter.9.cloned.1.call-start = ((), (), s32[]{:S(2)}) async-start(), calls=%async_computation.6 | async-start | bytes 98304 | tf_op jit(solution)/shard_map/reduce_scatter | solution.py:57
  163.9 29.0 %reduce-scatter.11.cloned.1.call-start = ((), (), s32[]{:S(2)}) async-start(), calls=%async_computation.7 | async-start | bytes 163840 | tf_op jit(solution)/shard_map/reduce_scatter | solution.py:60
Sparse Core Ops, SparseCore 0:
  36.9 11.1 reduce-scatter.4
  50.3 19.4 reduce-scatter.6
  164.0 7.3 reduce-scatter.8
  173.5 19.4 reduce-scatter.10
